TPU v7x, 32 devices: a whole 2x2x4 slice. The times are simulated.
32 devices in a mesh: fsdp: 8 (over z, x), tensor: 4 (over y, core).
Axes of the slice: x: 2, y: 2, z: 4, core: 2. Of those that a mesh axis runs over, the one named last changes fastest.
Arguments:
- hidden_in: bfloat16 [4096, 2048], P(('fsdp', 'tensor')), may hold values from -6 to 6
- ln_gain: float32 [2048], replicated, may hold values from 0.5 to 1.5
- ln_bias: float32 [2048], replicated, may hold values from -1.75 to 1.75
- w_qkv: bfloat16 [2048, 3, 2048], P('fsdp', None, 'tensor'), may hold values from -0.125 to 0.125
- b_qkv: float32 [3, 2048], P(None, 'tensor'), may hold values from -1.75 to 1.75
- w_dense: bfloat16 [2048, 2048], P('tensor', 'fsdp'), may hold values from -0.5 to 0.5
- b_dense: float32 [2048], replicated, may hold values from -1.75 to 1.75
- w_fc1: bfloat16 [2048, 8192], P('fsdp', 'tensor'), may hold values from -0.125 to 0.125
- b_fc1: float32 [8192], P('tensor'), may hold values from -1.75 to 1.75
- w_fc2: bfloat16 [8192, 2048], P('tensor', 'fsdp'), may hold values from -0.0625 to 0.0625
- b_fc2: float32 [2048], replicated, may hold values from -1.75 to 1.75
- segment_ids: int32 [8, 512], P('fsdp'), may hold values from 0 to 7, never falling along the last dimension, each value on 1 to 256 neighbouring positions
- out_grad: bfloat16 [4096, 2048], P(('fsdp', 'tensor')), may hold values from -6 to 6
Outputs:
- hidden_out: bfloat16 [4096, 2048], P(('fsdp', 'tensor'))
- input_grad: float32 [4096, 2048], P(('fsdp', 'tensor'))
- ln_gain_grad: float32 [2048], replicated
- ln_bias_grad: float32 [2048], replicated
- w_qkv_grad: float32 [2048, 3, 2048], P('fsdp', None, 'tensor')
- b_qkv_grad: float32 [3, 2048], P(None, 'tensor')
- w_dense_grad: float32 [2048, 2048], P('tensor', 'fsdp')
- b_dense_grad: float32 [2048], replicated
- w_fc1_grad: float32 [2048, 8192], P('fsdp', 'tensor')
- b_fc1_grad: float32 [8192], P('tensor')
- w_fc2_grad: float32 [8192, 2048], P('tensor', 'fsdp')
- b_fc2_grad: float32 [2048], replicated
Inputs may be any that keep to these rules, and one draw needn't show every extreme that they name: `segment_ids`: in each sequence the document numbers never fall; each document has 1 to 256 tokens and one has exactly 256.
All inputs are finite; a program needn't handle non-finite values.
Results may differ from a plain program's by a relative error of at most 0.0093.
Values may be sent and summed in bfloat16 or wider, within the bound.
No kernel may reach another device: no remote copies, remote signals or barrier semaphores. Data moves between devices by JAX's collectives and lax.ppermute only.
A program may use at most 192 MiB of HBM per device.

v0:
```python
import math
import jax
import jax.numpy as jnp
from jax import lax
from jax.sharding import PartitionSpec as P

HEAD_DIM = 64
ROT = 32
EPS = 1e-05


def layer_norm(values, norm_gain, norm_shift):
    centred = values - jnp.mean(values, axis=-1, keepdims=True)
    variance = jnp.mean(centred * centred, axis=-1, keepdims=True)
    return centred * lax.rsqrt(variance + EPS) * norm_gain + norm_shift


def gelu_tanh(values):
    return jax.nn.gelu(values, approximate=True)


def rotary_tables(length):
    positions = jnp.arange(length).astype(jnp.float32)
    inverse = 10000.0 ** (-jnp.arange(0, ROT, 2).astype(jnp.float32) / ROT)
    angles = positions[:, None] * inverse[None, :]
    return (jnp.cos(angles), jnp.sin(angles))


def rotate(values, cosine_rows, sine_rows):
    half_rot = ROT // 2
    first_half = values[..., :half_rot]
    second = values[..., half_rot:ROT]
    others = values[..., ROT:]
    cos_rows = cosine_rows[:, None, :]
    sin_rows = sine_rows[:, None, :]
    return jnp.concatenate(
        [
            first_half * cos_rows - second * sin_rows,
            second * cos_rows + first_half * sin_rows,
            others,
        ],
        axis=-1,
    )


def unrotate(values, cosine_rows, sine_rows):
    half_rot = ROT // 2
    first_half = values[..., :half_rot]
    second = values[..., half_rot:ROT]
    others = values[..., ROT:]
    cos_rows = cosine_rows[:, None, :]
    sin_rows = sine_rows[:, None, :]
    return jnp.concatenate(
        [
            first_half * cos_rows + second * sin_rows,
            second * cos_rows - first_half * sin_rows,
            others,
        ],
        axis=-1,
    )


def contract_rows(left, right):
    return lax.dot_general(
        left, right, (((0,), (0,)), ((), ())), preferred_element_type=jnp.float32
    )


def contract_cols(left, right):
    return lax.dot_general(
        left, right, (((1,), (1,)), ((), ())), preferred_element_type=jnp.float32
    )


def body(
    hidden_in,
    ln_gain,
    ln_bias,
    w_qkv,
    b_qkv,
    w_dense,
    b_dense,
    w_fc1,
    b_fc1,
    w_fc2,
    b_fc2,
    segment_ids,
    out_grad,
):
    hidden = hidden_in.astype(jnp.float32)
    normed = layer_norm(hidden, ln_gain, ln_bias)
    normed_all = lax.all_gather(normed.astype(jnp.bfloat16), "tensor", axis=0, tiled=True)
    seq_len = normed_all.shape[0]
    qkv_weights, up_weights = (
        lax.all_gather(w_qkv, "fsdp", axis=0, tiled=True),
        lax.all_gather(w_fc1, "fsdp", axis=0, tiled=True),
    )
    local_width = b_qkv.shape[1]
    head_count = local_width // HEAD_DIM
    mixed_proj = (
        jnp.einsum("sd,djc->sjc", normed_all, qkv_weights, preferred_element_type=jnp.float32)
        + b_qkv
    )
    before = jnp.dot(normed_all, up_weights, preferred_element_type=jnp.float32) + b_fc1
    cosine_rows, sine_rows = rotary_tables(seq_len)
    split_heads = mixed_proj.reshape(seq_len, 3, head_count, HEAD_DIM)
    queries = rotate(split_heads[:, 0], cosine_rows, sine_rows).astype(jnp.bfloat16)
    key_rows = rotate(split_heads[:, 1], cosine_rows, sine_rows).astype(jnp.bfloat16)
    value_rows = split_heads[:, 2].astype(jnp.bfloat16)
    segments = segment_ids[0]
    block_rows = min(512, seq_len)
    block_count = seq_len // block_rows
    score_scale = 1.0 / math.sqrt(HEAD_DIM)
    col_pos = jnp.arange(seq_len, dtype=jnp.int32)

    def block_scores(offset):
        row_pos = offset + jnp.arange(block_rows, dtype=jnp.int32)
        allowed = (col_pos[None, :] <= row_pos[:, None]) & (segments[:, None] == segments[None, :])
        scores = (
            jnp.einsum("qhd,khd->hqk", queries, key_rows, preferred_element_type=jnp.float32)
            * score_scale
        )
        return (queries, jnp.where(allowed[None], scores, -1e30))

    def forward_block(block_index):
        offset = block_index * block_rows
        query_rows, scores = block_scores(offset)
        highest = jnp.max(scores, axis=-1, keepdims=True)
        shifted = jnp.exp(scores - highest)
        totals = jnp.sum(shifted, axis=-1, keepdims=True)
        attend = (shifted / totals).astype(jnp.bfloat16)
        context = jnp.einsum("hqk,khd->qhd", attend, value_rows, preferred_element_type=jnp.float32)
        return (context, (highest + jnp.log(totals))[..., 0])

    contexts, log_sums = lax.map(forward_block, jnp.arange(block_count, dtype=jnp.int32))
    context_b = contexts.reshape(seq_len, local_width).astype(jnp.bfloat16)
    activated_b = gelu_tanh(before).astype(jnp.bfloat16)
    out_weights, down_weights = (
        lax.all_gather(w_dense, "fsdp", axis=1, tiled=True),
        lax.all_gather(w_fc2, "fsdp", axis=1, tiled=True),
    )
    attn_part = jnp.dot(context_b, out_weights, preferred_element_type=jnp.float32)
    mlp_part = jnp.dot(activated_b, down_weights, preferred_element_type=jnp.float32)
    branch_total = lax.psum_scatter(
        attn_part, "tensor", scatter_dimension=0, tiled=True
    ) + lax.psum_scatter(
        mlp_part.astype(jnp.bfloat16), "tensor", scatter_dimension=0, tiled=True
    ).astype(
        jnp.float32
    )
    hidden_out = (hidden + branch_total + b_dense + b_fc2).astype(jnp.bfloat16)
    grad_all = lax.all_gather(out_grad, "tensor", axis=0, tiled=True)
    dense_grad_local = contract_rows(context_b, grad_all)
    down_grad_local = contract_rows(activated_b, grad_all)
    dense_weight_grad, down_weight_grad = (
        lax.psum_scatter(dense_grad_local, "fsdp", scatter_dimension=1, tiled=True),
        lax.psum_scatter(down_grad_local, "fsdp", scatter_dimension=1, tiled=True),
    )
    context_grad = contract_cols(grad_all, out_weights).astype(jnp.bfloat16)
    activated_grad = contract_cols(grad_all, down_weights)
    gelu_value, gelu_pull = jax.vjp(gelu_tanh, before)
    before_grad = gelu_pull(activated_grad)[0].astype(jnp.bfloat16)
    up_grad_local = contract_rows(normed_all, before_grad)
    context_heads = context_grad.reshape(seq_len, head_count, HEAD_DIM)

    def backward_block(accumulate, block_index):
        key_acc, value_acc = accumulate
        offset = block_index * block_rows
        query_rows, scores = block_scores(offset)
        log_sum = lax.dynamic_index_in_dim(log_sums, block_index, 0, keepdims=False)
        attend = jnp.exp(scores - log_sum[..., None])
        attend_grad = jnp.einsum(
            "qhd,khd->hqk", context_heads, value_rows, preferred_element_type=jnp.float32
        )
        row_inner = jnp.sum(attend * attend_grad, axis=-1, keepdims=True)
        score_grad = (attend * (attend_grad - row_inner)).astype(jnp.bfloat16)
        query_grad = (
            jnp.einsum("hqk,khd->qhd", score_grad, key_rows, preferred_element_type=jnp.float32)
            * score_scale
        )
        key_acc = (
            key_acc
            + jnp.einsum("hqk,qhd->khd", score_grad, query_rows, preferred_element_type=jnp.float32)
            * score_scale
        )
        value_acc = value_acc + jnp.einsum(
            "hqk,qhd->khd",
            attend.astype(jnp.bfloat16),
            context_heads,
            preferred_element_type=jnp.float32,
        )
        return ((key_acc, value_acc), query_grad)

    zero_heads = jnp.zeros((seq_len, head_count, HEAD_DIM), jnp.float32)
    (key_grad, value_grad), query_grads = lax.scan(
        backward_block, (zero_heads, zero_heads), jnp.arange(block_count, dtype=jnp.int32)
    )
    query_grad = query_grads.reshape(seq_len, head_count, HEAD_DIM)
    mixed_grad = jnp.stack(
        [
            unrotate(query_grad, cosine_rows, sine_rows),
            unrotate(key_grad, cosine_rows, sine_rows),
            value_grad,
        ],
        axis=1,
    )
    mixed_grad = mixed_grad.reshape(seq_len, 3, local_width).astype(jnp.bfloat16)
    qkv_grad_local = jnp.einsum(
        "sd,sjc->djc", normed_all, mixed_grad, preferred_element_type=jnp.float32
    )
    attn_back = jnp.einsum(
        "sjc,djc->sd", mixed_grad, qkv_weights, preferred_element_type=jnp.float32
    )
    mlp_back = contract_cols(before_grad, up_weights)
    normed_grad = lax.psum_scatter(
        attn_back, "tensor", scatter_dimension=0, tiled=True
    ) + lax.psum_scatter(
        mlp_back.astype(jnp.bfloat16), "tensor", scatter_dimension=0, tiled=True
    ).astype(
        jnp.float32
    )
    norm_value, norm_pull = jax.vjp(layer_norm, hidden, ln_gain, ln_bias)
    hidden_grad, gain_local, shift_local = norm_pull(normed_grad)
    cotangent = out_grad.astype(jnp.float32)
    input_grad = cotangent + hidden_grad
    gain_grad, shift_grad, out_bias_grad = lax.psum(
        (gain_local, shift_local, jnp.sum(cotangent, axis=0)), ("fsdp", "tensor")
    )
    qkv_bias_grad, up_bias_grad = lax.psum(
        (
            jnp.sum(mixed_grad, axis=0, dtype=jnp.float32),
            jnp.sum(before_grad, axis=0, dtype=jnp.float32),
        ),
        "fsdp",
    )
    qkv_weight_grad, up_weight_grad = (
        lax.psum_scatter(qkv_grad_local, "fsdp", scatter_dimension=0, tiled=True),
        lax.psum_scatter(up_grad_local, "fsdp", scatter_dimension=0, tiled=True),
    )
    return (
        hidden_out,
        input_grad,
        gain_grad,
        shift_grad,
        qkv_weight_grad,
        qkv_bias_grad,
        dense_weight_grad,
        out_bias_grad,
        up_weight_grad,
        up_bias_grad,
        down_weight_grad,
        out_bias_grad,
    )


def solution(mesh):
    in_specs = (
        P(("fsdp", "tensor"), None),
        P(),
        P(),
        P("fsdp", None, "tensor"),
        P(None, "tensor"),
        P("tensor", "fsdp"),
        P(),
        P("fsdp", "tensor"),
        P("tensor"),
        P("tensor", "fsdp"),
        P(),
        P("fsdp", None),
        P(("fsdp", "tensor"), None),
    )
    out_specs = (
        P(("fsdp", "tensor"), None),
        P(("fsdp", "tensor"), None),
        P(),
        P(),
        P("fsdp", None, "tensor"),
        P(None, "tensor"),
        P("tensor", "fsdp"),
        P(),
        P("fsdp", "tensor"),
        P("tensor"),
        P("tensor", "fsdp"),
        P(),
    )
    return jax.shard_map(body, mesh=mesh, in_specs=in_specs, out_specs=out_specs, check_vma=False)
```

profile of v0, /device:TPU:0, one launch (start us, length us, event | category | flops | bytes accessed | tf_op | source)
XLA Modules:
  0.0 1531.4 jit_solution(14621272679159537273)
XLA Ops:
  19.9 15.0 all-gather.17.cloned.1.call-done
  34.9 53.2 %all-gather.11.cloned.1.call-done = bf16[512,2048]{1,0:T(8,128)(2,1)} async-done(((bf16[512,256]{1,0:T(8,128)(2,1)}), bf16[512,2048]{1,0:T(8,128)(2,1)}) %all-gather.11.cloned.1.call-update) | async-done | bytes 2097168 | tf_op jit(solution)/shard_map/all_gather | solution.py:139
  88.1 4.3 convolution_convert_fusion.2
  92.4 18.7 %all-gather.7.cloned.1.call-done = bf16[512,2048]{1,0:T(8,128)(2,1)} async-done(((bf16[128,2048]{1,0:T(8,128)(2,1)}), bf16[512,2048]{1,0:T(8,128)(2,1)}) %all-gather.7.cloned.1.call-update) | async-done | bytes 2097168 | tf_op jit(solution)/shard_map/all_gather | solution.py:92
  111.1 102.4 %all-gather.9.cloned.1.call-done = bf16[2048,3,512]{0,2,1:T(8,128)(2,1)} async-done(((bf16[256,3,512]{0,2,1:T(8,128)(2,1)}), bf16[2048,3,512]{0,2,1:T(8,128)(2,1)}) %all-gather.9.cloned.1.call-update) | async-done | bytes 6291472 | tf_op jit(solution)/shard_map/all_gather | solution.py:95
  213.5 6.7 fusion.17
  221.9 4.7 fusion.53
  226.6 111.9 %all-gather.13.cloned.1.call-done = bf16[2048,2048]{1,0:T(8,128)(2,1)} async-done(((bf16[256,2048]{1,0:T(8,128)(2,1)}), bf16[2048,2048]{1,0:T(8,128)(2,1)}) %all-gather.13.cloned.1.call-update) | async-done | bytes 8388624 | tf_op jit(solution)/shard_map/all_gather | solution.py:96
  338.5 10.5 fusion.55
  349.0 115.0 %all-gather.15.cloned.1.call-done = bf16[2048,2048]{1,0:T(8,128)(2,1)} async-done(((bf16[2048,256]{1,0:T(8,128)(2,1)}), bf16[2048,2048]{1,0:T(8,128)(2,1)}) %all-gather.15.cloned.1.call-update) | async-done | bytes 8388624 | tf_op jit(solution)/shard_map/all_gather | solution.py:140
  464.0 12.8 convert_reduce_fusion
  478.2 5.9 convolution_convert_fusion
  484.2 4.7 fusion
  490.6 3.3 fusion.27
  496.0 4.6 multiply_reduce_fusion
  500.6 4.5 multiply_convert_fusion
  512.8 8.8 convolution_bitcast_fusion
  522.3 11.8 convolution_convert_fusion.1
  534.2 5.0 fusion.26
  540.0 3.2 fusion.54
  544.3 4.8 fusion.56
  549.2 8.1 fusion.13
  557.7 14.1 fusion.50
  571.9 12.8 fusion.57
  585.3 35.0 %all-reduce.1 = (f32[3,512]{1,0:T(4,128)}, f32[2048]{0:T(1024)}) all-reduce(f32[3,512]{1,0:T(4,128)S(1)} %convert_reduce_fusion.1, f32[2048]{0:T(1024)S(1)} %copy-done.32), channel_id=1, replica_groups=mesh['fsdp'=8,'tensor'=4] {'fsdp'}, use_global_device_ids=true, to_apply=%region_17.18 | all-reduce | flops 3584 | bytes 28672 | tf_op jit(solution)/shard_map/psum | solution.py:229
  622.3 23.2 %reduce-scatter.9.cloned.1.call-done = f32[128,2048]{1,0:T(8,128)} async-done(((f32[512,2048]{1,0:T(8,128)}), f32[128,2048]{1,0:T(8,128)}) %reduce-scatter.9.cloned.1.call-update) | async-done | bytes 1048592 | tf_op jit(solution)/shard_map/reduce_scatter | solution.py:144
  645.4 3.2 fusion.52
  649.9 41.7 %all-reduce = (f32[2048]{0:T(1024)}, f32[2048]{0:T(1024)}, f32[2048]{0:T(1024)S(1)}) all-reduce(f32[2048]{0:T(1024)S(1)} %get-tuple-element.58, f32[2048]{0:T(1024)S(1)} %get-tuple-element.60, f32[2048]{0:T(1024)S(1)} %get-tuple-element.91), channel_id=1, replica_groups=mesh['fsdp'=8,'tensor'=4] {'fsdp','tensor'}, use_global_device_ids=true, to_apply=%region_12.13 | all-reduce | flops 6144 | bytes 49152 | tf_op jit(solution)/shard_map/psum | solution.py:226
  691.6 47.6 %reduce-scatter.19.cloned.1.call-done = f32[512,256]{1,0:T(8,128)} async-done(((f32[512,2048]{1,0:T(8,128)}), f32[512,256]{1,0:T(8,128)}) %reduce-scatter.19.cloned.1.call-update) | async-done | bytes 524304 | tf_op jit(solution)/shard_map/reduce_scatter | solution.py:156
  739.2 212.0 %reduce-scatter.17.cloned.1.call-done = f32[256,3,512]{2,0,1:T(8,128)} async-done(((f32[2048,3,512]{2,0,1:T(8,128)}), f32[256,3,512]{2,0,1:T(8,128)}) %reduce-scatter.17.cloned.1.call-update) | async-done | bytes 1572880 | tf_op jit(solution)/shard_map/reduce_scatter | solution.py:237
  951.2 286.7 %reduce-scatter.23.cloned.1.call-done = f32[2048,256]{1,0:T(8,128)} async-done(((f32[2048,2048]{1,0:T(8,128)}), f32[2048,256]{1,0:T(8,128)}) %reduce-scatter.23.cloned.1.call-update) | async-done | bytes 2097168 | tf_op jit(solution)/shard_map/reduce_scatter | solution.py:157
  1237.9 286.0 %reduce-scatter.21.cloned.1.call-done = f32[256,2048]{1,0:T(8,128)} async-done(((f32[2048,2048]{1,0:T(8,128)}), f32[256,2048]{1,0:T(8,128)}) %reduce-scatter.21.cloned.1.call-update) | async-done | bytes 2097168 | tf_op jit(solution)/shard_map/reduce_scatter | solution.py:238
  (145 shorter events, 34.1 us)
Async XLA Ops:
  7.2 11.8 copy-start.31
  7.2 27.7 %all-gather.17.cloned.1.call-start = ((), (), s32[]{:S(2)}) async-start(), calls=%async_computation.15 | async-start | bytes 2621440 | tf_op jit(solution)/shard_map/all_gather | solution.py:152
  7.9 80.2 %all-gather.11.cloned.1.call-start = ((), (), s32[]{:S(2)}) async-start(), calls=%async_computation.10 | async-start | bytes 2359296 | tf_op jit(solution)/shard_map/all_gather | solution.py:139
  8.7 102.4 %all-gather.7.cloned.1.call-start = ((), (), s32[]{:S(2)}) async-start(), calls=%async_computation.8 | async-start | bytes 2621440 | tf_op jit(solution)/shard_map/all_gather | solution.py:92
  14.6 198.9 %all-gather.9.cloned.1.call-start = ((), (), s32[]{:S(2)}) async-start(), calls=%async_computation.9 | async-start | bytes 7077888 | tf_op jit(solution)/shard_map/all_gather | solution.py:95
  16.9 321.6 %all-gather.13.cloned.1.call-start = ((), (), s32[]{:S(2)}) async-start(), calls=%async_computation.12 | async-start | bytes 9437184 | tf_op jit(solution)/shard_map/all_gather | solution.py:96
  17.5 196.0 %copy-start.39 = (f32[3,512]{1,0:T(4,128)S(1)}, f32[3,512]{1,0:T(4,128)}, u32[]{:S(2)}) copy-start(f32[3,512]{1,0:T(4,128)} %param.17) | copy-start | bytes 18436
  17.5 446.5 %all-gather.15.cloned.1.call-start = ((), (), s32[]{:S(2)}) async-start(), calls=%async_computation.13 | async-start | bytes 9437184 | tf_op jit(solution)/shard_map/all_gather | solution.py:140
  18.1 602.2 %reduce-scatter.15.cloned.1.call-start = ((), (), s32[]{:S(2)}) async-start(), calls=%async_computation.17 | async-start | bytes 2621440 | tf_op jit(solution)/shard_map/reduce_scatter | solution.py:217
  226.6 257.6 %copy-start.23 = (f32[8,512]{1,0:T(8,128)}, f32[8,512]{1,0:T(8,128)S(1)}, u32[]{:S(2)}) copy-start(f32[8,512]{1,0:T(8,128)S(1)} %get-tuple-element.100) | copy-start | bytes 49156
  464.0 14.2 copy-start.38
  484.2 136.2 %reduce-scatter.13.cloned.1.call-start = ((), (), s32[]{:S(2)}) async-start(), calls=%async_computation.16 | async-start | bytes 5242880 | tf_op jit(solution)/shard_map/reduce_scatter | solution.py:215
  484.2 6.4 copy-start
  521.7 12.5 copy-start.24
  521.7 12.5 copy-start.26
  521.7 100.6 %reduce-scatter.11.cloned.1.call-start = ((), (), s32[]{:S(2)}) async-start(), calls=%async_computation.14 | async-start | bytes 2621440 | tf_op jit(solution)/shard_map/reduce_scatter | solution.py:146
  534.1 111.3 %reduce-scatter.9.cloned.1.call-start = ((), (), s32[]{:S(2)}) async-start(), calls=%async_computation.11 | async-start | bytes 5242880 | tf_op jit(solution)/shard_map/reduce_scatter | solution.py:144
  543.3 5.9 copy-start.2
  543.3 5.9 copy-start.3
  543.3 195.9 %reduce-scatter.19.cloned.1.call-start = ((), (), s32[]{:S(2)}) async-start(), calls=%async_computation.19 | async-start | bytes 4718592 | tf_op jit(solution)/shard_map/reduce_scatter | solution.py:156
  549.2 402.1 %reduce-scatter.17.cloned.1.call-start = ((), (), s32[]{:S(2)}) async-start(), calls=%async_computation.18 | async-start | bytes 14155776 | tf_op jit(solution)/shard_map/reduce_scatter | solution.py:237
  557.4 680.5 %reduce-scatter.23.cloned.1.call-start = ((), (), s32[]{:S(2)}) async-start(), calls=%async_computation.21 | async-start | bytes 18874368 | tf_op jit(solution)/shard_map/reduce_scatter | solution.py:157
  571.8 952.0 %reduce-scatter.21.cloned.1.call-start = ((), (), s32[]{:S(2)}) async-start(), calls=%async_computation.20 | async-start | bytes 18874368 | tf_op jit(solution)/shard_map/reduce_scatter | solution.py:238
  584.6 35.7 %copy-start.1 = (bf16[128,2048]{1,0:T(8,128)(2,1)S(1)}, bf16[128,2048]{1,0:T(8,128)(2,1)}, u32[]{:S(2)}) copy-start(bf16[128,2048]{1,0:T(8,128)(2,1)} %param.13) | copy-start | bytes 1572868
  584.6 35.7 %copy-start.22 = (f32[2048]{0:T(1024)S(1)}, f32[2048]{0:T(1024)}, u32[]{:S(2)}) copy-start(f32[2048]{0:T(1024)} %param.14) | copy-start | bytes 24580
  584.7 35.7 %copy-start.28 = (f32[128]{0:T(128)S(1)}, f32[128]{0:T(128)}, u32[]{:S(2)}) copy-start(f32[128]{0:T(128)} %copy-done.27) | copy-start | bytes 1540
  584.7 35.7 %copy-start.35 = (f32[128]{0:T(128)S(1)}, f32[128]{0:T(128)}, u32[]{:S(2)}) copy-start(f32[128]{0:T(128)} %copy-done.34) | copy-start | bytes 1540
  584.7 37.5 %copy-start.37 = (f32[128]{0:T(128)S(1)}, f32[128]{0:T(128)}, u32[]{:S(2)}) copy-start(f32[128]{0:T(128)} %copy-done.36) | copy-start | bytes 1540
  584.7 60.8 %copy-start.29 = (f32[2048]{0:T(1024)S(1)}, f32[2048]{0:T(1024)}, u32[]{:S(2)}) copy-start(f32[2048]{0:T(1024)} %param.23) | copy-start | bytes 24580
  584.7 60.8 %copy-start.30 = (f32[2048]{0:T(1024)S(1)}, f32[2048]{0:T(1024)}, u32[]{:S(2)}) copy-start(f32[2048]{0:T(1024)} %param.19) | copy-start | bytes 24580
  584.7 63.9 %copy-start.6 = (bf16[128,2048]{1,0:T(8,128)(2,1)S(1)}, bf16[128,2048]{1,0:T(8,128)(2,1)}, u32[]{:S(2)}) copy-start(bf16[128,2048]{1,0:T(8,128)(2,1)} %param.25) | copy-start | bytes 1572868
  691.6 832.9 %copy-start.33 = (f32[2048]{0:T(1024)}, f32[2048]{0:T(1024)S(1)}, u32[]{:S(2)}) copy-start(f32[2048]{0:T(1024)S(1)} %get-tuple-element.129) | copy-start | bytes 24580
  (24 other events, 47.7 us)
Sparse Core Ops, SparseCore 0:
  9.6 25.2 all-gather.16
  36.9 51.1 all-gather.10
  90.3 20.7 all-gather.6
  113.5 99.9 all-gather.8
  215.5 123.0 all-gather.12
  340.4 123.5 all-gather.14
  484.3 29.5 reduce-scatter.14
  521.8 42.5 reduce-scatter.12
  566.9 31.4 reduce-scatter.10
  600.9 44.4 reduce-scatter.8
  649.7 89.4 reduce-scatter.18
  743.7 207.5 reduce-scatter.16
  956.1 281.7 reduce-scatter.22
  1242.1 281.7 reduce-scatter.20
where the time goes:
time: 1540 us; the launch traced here: 1530 us
  waiting for transfers between devices  1270 us (82%)
  matrix products  124 us (8%)
  blocking collectives  76.7 us (5%)
  other arithmetic  25 us (2%)
  local copies, waits for them, and re-layouts  15.8 us (1%)
    reduce_scatter x1, waiting for transfers between devices, body(): lax.psum_scatter(down_grad_local, 'fsdp', scatter_dimension=1, tiled=True)  287 us
    reduce_scatter x1, waiting for transfers between devices, body(): lax.psum_scatter(up_grad_local, 'fsdp', scatter_dimension=0, tiled=True)  286 us
    reduce_scatter x1, waiting for transfers between devices, body(): lax.psum_scatter(qkv_grad_local, 'fsdp', scatter_dimension=0, tiled=True)  212 us
    all_gather x1, waiting for transfers between devices, body(): lax.all_gather(w_fc2, 'fsdp', axis=1, tiled=True)  115 us
    all_gather x1, waiting for transfers between devices, body(): lax.all_gather(w_fc1, 'fsdp', axis=0, tiled=True)  112 us
    all_gather x1, waiting for transfers between devices, body(): lax.all_gather(w_qkv, 'fsdp', axis=0, tiled=True)  102 us
    all_gather x1, waiting for transfers between devices, body(): lax.all_gather(w_dense, 'fsdp', axis=1, tiled=True)  53.2 us
    reduce_scatter x1, waiting for transfers between devices, body(): lax.psum_scatter(dense_grad_local, 'fsdp', scatter_dimension=1, tiled=True)  47.6 us
  transfers between devices with their start and end apart: 14, of which 11 were waited for; matrix products, arithmetic and copies ran while one was open for 9% of the time, Pallas kernels for 0%

commit v1 on v0

--- a/solution.py
+++ b/solution.py
@@ -7,6 +7,33 @@
 HEAD_DIM = 64
 ROT = 32
 EPS = 1e-05
+
+
+def report_cycles(xin, axis_name="fsdp"):
+    piece_now, plain, base_arr = (lax.psum(1, axis_name), lax.axis_index(axis_name), xin.shape[0])
+    value_now = lax.dynamic_update_slice_in_dim(
+        jnp.zeros(
+            tuple((kk * piece_now if ix == 0 else kk for ix, kk in enumerate(xin.shape))), xin.dtype
+        ),
+        xin,
+        plain * base_arr,
+        axis=0,
+    )
+    newest = after = xin
+    for num in range(1, piece_now // 2 + 1):
+        newest = lax.ppermute(
+            newest, axis_name, tuple(((ix, (ix + 1) % piece_now) for ix in range(piece_now)))
+        )
+        value_now = lax.dynamic_update_slice_in_dim(
+            value_now, newest, (plain - num) % piece_now * base_arr, axis=0
+        )
+        if 2 * num < piece_now:
+            prior = tuple(((ix, (ix - 1) % piece_now) for ix in range(piece_now)))
+            after = lax.ppermute(after, axis_name, prior)
+            value_now = lax.dynamic_update_slice_in_dim(
+                value_now, after, (plain + num) % piece_now * base_arr, axis=0
+            )
+    return value_now
 
 
 def layer_norm(values, norm_gain, norm_shift):
@@ -92,7 +119,7 @@
     normed_all = lax.all_gather(normed.astype(jnp.bfloat16), "tensor", axis=0, tiled=True)
     seq_len = normed_all.shape[0]
     qkv_weights, up_weights = (
-        lax.all_gather(w_qkv, "fsdp", axis=0, tiled=True),
+        report_cycles(w_qkv),
         lax.all_gather(w_fc1, "fsdp", axis=0, tiled=True),
     )
     local_width = b_qkv.shape[1]

time: 1540 us -> 1450 us (0.942)
  waiting for transfers between devices: 1270 us -> 1170 us
  starting transfers between devices: 1.03 us -> 21.2 us
    ppermute x0 -> x7, waiting for transfers between devices: none -> 114 us  [the longest x4 114 us: report_cycles(): lax.ppermute(newest, axis_name, tuple(((ix, (ix + 1) % piece_now) for ix...]
    all_gather x1 -> x0, waiting for transfers between devices: 102 us -> none  [body(): lax.all_gather(w_qkv, 'fsdp', axis=0, tiled=True)]
    all_gather x1, waiting for transfers between devices: 53.2 us -> 0.02 us  [body(): lax.all_gather(w_dense, 'fsdp', axis=1, tiled=True)]
    all_gather x1, waiting for transfers between devices: 112 us -> 62.4 us  [body(): lax.all_gather(w_fc1, 'fsdp', axis=0, tiled=True)]
    reduce_scatter x1, waiting for transfers between devices: 0.02 us -> 34.2 us  [body(): lax.psum_scatter(mlp_part.astype(jnp.bfloat16), 'tensor', scatter_dimensi...]
    ppermute x0 -> x7, starting transfers between devices: none -> 20.1 us  [the longest x4 10.9 us: report_cycles(): lax.ppermute(newest, axis_name, tuple(((ix, (ix + 1) % piece_now) for ix...]
    all_gather x1, waiting for transfers between devices: 18.7 us -> 0.01 us  [body(): lax.all_gather(normed.astype(jnp.bfloat16), 'tensor', axis=0, tiled=True)]
    reduce_scatter x1, waiting for transfers between devices: 23.2 us -> 7.52 us  [body(): lax.psum_scatter(attn_part, 'tensor', scatter_dimension=0, tiled=True)]
  transfers between devices with their start and end apart: 14 -> 20, of which waited for: 11 -> 12; matrix products, arithmetic and copies ran while one was open for 9% -> 11% of each run, Pallas kernels for 0% -> 0%
where the time goes in v1:
time: 1450 us
  waiting for transfers between devices  1170 us (81%)
  matrix products  121 us (8%)
  blocking collectives  77.2 us (5%)
  local copies, waits for them, and re-layouts  25.1 us (2%)
  starting transfers between devices  21.2 us (1%)
  other arithmetic  20.4 us (1%)
  between operations  14.7 us (1%)
    reduce_scatter x1, waiting for transfers between devices, body(): lax.psum_scatter(down_grad_local, 'fsdp', scatter_dimension=1, tiled=True)  287 us
    reduce_scatter x1, waiting for transfers between devices, body(): lax.psum_scatter(up_grad_local, 'fsdp', scatter_dimension=0, tiled=True)  286 us
    reduce_scatter x1, waiting for transfers between devices, body(): lax.psum_scatter(qkv_grad_local, 'fsdp', scatter_dimension=0, tiled=True)  212 us
    all_gather x1, waiting for transfers between devices, body(): lax.all_gather(w_fc2, 'fsdp', axis=1, tiled=True)  115 us
    ppermute x4, waiting for transfers between devices, report_cycles(): lax.ppermute(newest, axis_name, tuple(((ix, (ix + 1) % piece_now) for ix...  114 us
    all_gather x1, waiting for transfers between devices, body(): lax.all_gather(w_fc1, 'fsdp', axis=0, tiled=True)  62.4 us
    reduce_scatter x1, waiting for transfers between devices, body(): lax.psum_scatter(dense_grad_local, 'fsdp', scatter_dimension=1, tiled=True)  47.1 us
    psum x1, blocking collectives, body(): lax.psum((gain_local, shift_local, jnp.sum(cotangent, axis=0)), ('fsdp',...  41.9 us
  transfers between devices with their start and end apart: 20, of which 12 were waited for; matrix products, arithmetic and copies ran while one was open for 11% of the time, Pallas kernels for 0%

profile of v1, /device:TPU:0, one launch (start us, length us, event | category | flops | bytes accessed | tf_op | source)
XLA Modules:
  0.0 1447.0 jit_solution(16841329107066111813)
XLA Ops:
  21.5 30.5 %collective-permute-done = bf16[256,3,512]{2,0,1:T(8,128)(2,1)S(1)} collective-permute-done((bf16[256,3,512]{2,0,1:T(8,128)(2,1)S(1)}, bf16[256,3,512]{2,0,1:T(8,128)(2,1)S(1)}, u32[]{:S(2)}, u32[]{:S(2)}) %collective-permute-start) | collective-permute-done | bytes 786464 | tf_op jit(solution)/shard_map/ppermute | solution.py:24
  57.5 32.7 %collective-permute-done.2 = bf16[256,3,512]{2,0,1:T(8,128)(2,1)} collective-permute-done((bf16[256,3,512]{2,0,1:T(8,128)(2,1)S(1)}, bf16[256,3,512]{2,0,1:T(8,128)(2,1)}, u32[]{:S(2)}, u32[]{:S(2)}) %collective-permute-start.2) | collective-permute-done | bytes 786464 | tf_op jit(solution)/shard_map/ppermute | solution.py:24
  97.6 3.2 broadcast_in_dim.84
  101.7 34.6 %collective-permute-done.4 = bf16[256,3,512]{2,0,1:T(8,128)(2,1)S(1)} collective-permute-done((bf16[256,3,512]{2,0,1:T(8,128)(2,1)}, bf16[256,3,512]{2,0,1:T(8,128)(2,1)S(1)}, u32[]{:S(2)}, u32[]{:S(2)}) %collective-permute-start.4) | collective-permute-done | bytes 786464 | tf_op jit(solution)/shard_map/ppermute | solution.py:24
  146.0 16.0 %collective-permute-done.6 = bf16[256,3,512]{2,0,1:T(8,128)(2,1)S(1)} collective-permute-done((bf16[256,3,512]{2,0,1:T(8,128)(2,1)S(1)}, bf16[256,3,512]{2,0,1:T(8,128)(2,1)S(1)}, u32[]{:S(2)}, u32[]{:S(2)}) %collective-permute-start.6) | collective-permute-done | bytes 786464 | tf_op jit(solution)/shard_map/ppermute | solution.py:24
  163.0 6.3 fusion.17
  175.8 3.5 convolution_convert_fusion.2
  179.4 5.8 fusion.27
  187.3 4.6 multiply_reduce_fusion
  192.0 4.7 multiply_convert_fusion
  204.5 8.7 convolution_bitcast_fusion
  213.3 62.4 %all-gather.10.cloned.1.call-done = bf16[2048,2048]{1,0:T(8,128)(2,1)} async-done(((bf16[256,2048]{1,0:T(8,128)(2,1)}), bf16[2048,2048]{1,0:T(8,128)(2,1)}) %all-gather.10.cloned.1.call-update) | async-done | bytes 8388624 | tf_op jit(solution)/shard_map/all_gather | solution.py:123
  275.7 10.5 fusion.55
  286.2 115.0 %all-gather.12.cloned.1.call-done = bf16[2048,2048]{1,0:T(8,128)(2,1)} async-done(((bf16[2048,256]{1,0:T(8,128)(2,1)}), bf16[2048,2048]{1,0:T(8,128)(2,1)}) %all-gather.12.cloned.1.call-update) | async-done | bytes 8388624 | tf_op jit(solution)/shard_map/all_gather | solution.py:167
  401.2 12.2 convert_reduce_fusion
  414.8 5.8 convolution_convert_fusion
  421.1 5.0 fusion.26
  426.9 3.3 fusion.54
  430.3 11.1 convolution_convert_fusion.1
  441.4 5.0 fusion.56
  446.5 8.3 fusion.13
  455.1 14.7 %fusion.50 = f32[2048,2048]{1,0:T(8,128)} fusion(bf16[512,2048]{1,0:T(8,128)(2,1)} %all-gather.14.cloned.1.call-done, f32[512,2048]{1,0:T(8,128)} %fusion.55, f32[2048]{0:T(1024)S(1)} %copy-done.41), kind=kOutput, calls=%fused_computation.105 | convolution fusion | flops 4305453056 | bytes 23076864 | tf_op jit(solution)/shard_map/dot_general | solution.py:91
  469.9 12.5 fusion.57
  482.7 35.4 %all-reduce.1 = (f32[3,512]{1,0:T(4,128)}, f32[2048]{0:T(1024)}) all-reduce(f32[3,512]{1,0:T(4,128)S(1)} %convert_reduce_fusion.1, f32[2048]{0:T(1024)S(1)} %get-tuple-element.77), channel_id=1, replica_groups=mesh['fsdp'=8,'tensor'=4] {'fsdp'}, use_global_device_ids=true, to_apply=%region_17.18 | all-reduce | flops 3584 | bytes 28672 | tf_op jit(solution)/shard_map/psum | solution.py:256
  520.0 7.5 reduce-scatter.9.cloned.1.call-done
  527.5 34.2 %reduce-scatter.11.cloned.1.call-done = bf16[128,2048]{1,0:T(8,128)(2,1)} async-done(((bf16[512,2048]{1,0:T(8,128)(2,1)}), bf16[128,2048]{1,0:T(8,128)(2,1)}) %reduce-scatter.11.cloned.1.call-update) | async-done | bytes 524304 | tf_op jit(solution)/shard_map/reduce_scatter | solution.py:173
  561.7 3.2 fusion.52
  566.1 41.9 %all-reduce = (f32[2048]{0:T(1024)}, f32[2048]{0:T(1024)}, f32[2048]{0:T(1024)S(1)}) all-reduce(f32[2048]{0:T(1024)S(1)} %get-tuple-element.58, f32[2048]{0:T(1024)S(1)} %get-tuple-element.60, f32[2048]{0:T(1024)S(1)} %get-tuple-element.91), channel_id=1, replica_groups=mesh['fsdp'=8,'tensor'=4] {'fsdp','tensor'}, use_global_device_ids=true, to_apply=%region_12.13 | all-reduce | flops 6144 | bytes 49152 | tf_op jit(solution)/shard_map/psum | solution.py:253
  608.0 47.1 %reduce-scatter.19.cloned.1.call-done = f32[512,256]{1,0:T(8,128)} async-done(((f32[512,2048]{1,0:T(8,128)}), f32[512,256]{1,0:T(8,128)}) %reduce-scatter.19.cloned.1.call-update) | async-done | bytes 524304 | tf_op jit(solution)/shard_map/reduce_scatter | solution.py:183
  655.1 212.1 %reduce-scatter.17.cloned.1.call-done = f32[256,3,512]{2,0,1:T(8,128)} async-done(((f32[2048,3,512]{2,0,1:T(8,128)}), f32[256,3,512]{2,0,1:T(8,128)}) %reduce-scatter.17.cloned.1.call-update) | async-done | bytes 1572880 | tf_op jit(solution)/shard_map/reduce_scatter | solution.py:264
  867.2 286.5 %reduce-scatter.23.cloned.1.call-done = f32[2048,256]{1,0:T(8,128)} async-done(((f32[2048,2048]{1,0:T(8,128)}), f32[2048,256]{1,0:T(8,128)}) %reduce-scatter.23.cloned.1.call-update) | async-done | bytes 2097168 | tf_op jit(solution)/shard_map/reduce_scatter | solution.py:184
  1153.7 286.0 %reduce-scatter.21.cloned.1.call-done = f32[256,2048]{1,0:T(8,128)} async-done(((f32[2048,2048]{1,0:T(8,128)}), f32[256,2048]{1,0:T(8,128)}) %reduce-scatter.21.cloned.1.call-update) | async-done | bytes 2097168 | tf_op jit(solution)/shard_map/reduce_scatter | solution.py:265
  (166 shorter events, 61.9 us)
Async XLA Ops:
  7.2 86.5 %copy-start.33 = (s32[1,512]{1,0:T(1,128)S(1)}, s32[1,512]{1,0:T(1,128)}, u32[]{:S(2)}) copy-start(s32[1,512]{1,0:T(1,128)} %param.24) | copy-start | bytes 6148
  7.2 155.8 %all-gather.6.cloned.1.call-start = ((), (), s32[]{:S(2)}) async-start(), calls=%async_computation.8 | async-start | bytes 2621440 | tf_op jit(solution)/shard_map/all_gather | solution.py:119
  12.7 163.1 %all-gather.14.cloned.1.call-start = ((), (), s32[]{:S(2)}) async-start(), calls=%async_computation.14 | async-start | bytes 2621440 | tf_op jit(solution)/shard_map/all_gather | solution.py:179
  13.4 162.4 %all-gather.8.cloned.1.call-start = ((), (), s32[]{:S(2)}) async-start(), calls=%async_computation.9 | async-start | bytes 2359296 | tf_op jit(solution)/shard_map/all_gather | solution.py:166
  14.1 261.5 %all-gather.10.cloned.1.call-start = ((), (), s32[]{:S(2)}) async-start(), calls=%async_computation.11 | async-start | bytes 9437184 | tf_op jit(solution)/shard_map/all_gather | solution.py:123
  14.7 386.5 %all-gather.12.cloned.1.call-start = ((), (), s32[]{:S(2)}) async-start(), calls=%async_computation.12 | async-start | bytes 9437184 | tf_op jit(solution)/shard_map/all_gather | solution.py:167
  15.3 502.8 %reduce-scatter.13.cloned.1.call-start = ((), (), s32[]{:S(2)}) async-start(), calls=%async_computation.15 | async-start | bytes 5242880 | tf_op jit(solution)/shard_map/reduce_scatter | solution.py:242
  15.4 36.6 %collective-permute-start = (bf16[256,3,512]{2,0,1:T(8,128)(2,1)S(1)}, bf16[256,3,512]{2,0,1:T(8,128)(2,1)S(1)}, u32[]{:S(2)}, u32[]{:S(2)}) collective-permute-start(bf16[256,3,512]{2,0,1:T(8,128)(2,1)S(1)} %copy-done.12), channel_id=1, source_target_pairs={{0,4},{4,8},{8,12},{12,16},{16,20},{20,24},{24,28},{28,0},{1,5},{5... | collective-permute-start | bytes 2359304 | tf_op jit(solution)/shard_map/ppermute | solution.py:24
  18.4 36.1 %collective-permute-start.1 = (bf16[256,3,512]{2,0,1:T(8,128)(2,1)S(1)}, bf16[256,3,512]{2,0,1:T(8,128)(2,1)S(1)}, u32[]{:S(2)}, u32[]{:S(2)}) collective-permute-start(bf16[256,3,512]{2,0,1:T(8,128)(2,1)S(1)} %copy-done.12), channel_id=1, source_target_pairs={{0,28},{4,0},{8,4},{12,8},{16,12},{20,16},{24,20},{28,24},{1,29},{... | collective-permute-start | bytes 2359304 | tf_op jit(solution)/shard_map/ppermute | solution.py:32
  52.0 38.2 %collective-permute-start.2 = (bf16[256,3,512]{2,0,1:T(8,128)(2,1)S(1)}, bf16[256,3,512]{2,0,1:T(8,128)(2,1)}, u32[]{:S(2)}, u32[]{:S(2)}) collective-permute-start(bf16[256,3,512]{2,0,1:T(8,128)(2,1)S(1)} %collective-permute-done), channel_id=1, source_target_pairs={{0,4},{4,8},{8,12},{12,16},{16,20},{20,24},{24,28},{28,0},{1,5},{5... | collective-permute-start | bytes 2359304 | tf_op jit(solution)/shard_map/ppermute | solution.py:24
  54.5 40.1 %collective-permute-start.3 = (bf16[256,3,512]{2,0,1:T(8,128)(2,1)S(1)}, bf16[256,3,512]{2,0,1:T(8,128)(2,1)S(1)}, u32[]{:S(2)}, u32[]{:S(2)}) collective-permute-start(bf16[256,3,512]{2,0,1:T(8,128)(2,1)S(1)} %collective-permute-done.1), channel_id=1, source_target_pairs={{0,28},{4,0},{8,4},{12,8},{16,12},{20,16},{24,20},{28,24},{1,29},{... | collective-permute-start | bytes 2359304 | tf_op jit(solution)/shard_map/ppermute | solution.py:32
  90.2 46.1 %collective-permute-start.4 = (bf16[256,3,512]{2,0,1:T(8,128)(2,1)}, bf16[256,3,512]{2,0,1:T(8,128)(2,1)S(1)}, u32[]{:S(2)}, u32[]{:S(2)}) collective-permute-start(bf16[256,3,512]{2,0,1:T(8,128)(2,1)} %collective-permute-done.2), channel_id=1, source_target_pairs={{0,4},{4,8},{8,12},{12,16},{16,20},{20,24},{24,28},{28,0},{1,5},{5... | collective-permute-start | bytes 2359304 | tf_op jit(solution)/shard_map/ppermute | solution.py:24
  94.6 50.5 %collective-permute-start.5 = (bf16[256,3,512]{2,0,1:T(8,128)(2,1)S(1)}, bf16[256,3,512]{2,0,1:T(8,128)(2,1)S(1)}, u32[]{:S(2)}, u32[]{:S(2)}) collective-permute-start(bf16[256,3,512]{2,0,1:T(8,128)(2,1)S(1)} %collective-permute-done.3), channel_id=1, source_target_pairs={{0,28},{4,0},{8,4},{12,8},{16,12},{20,16},{24,20},{28,24},{1,29},{... | collective-permute-start | bytes 2359304 | tf_op jit(solution)/shard_map/ppermute | solution.py:32
  136.3 25.7 %collective-permute-start.6 = (bf16[256,3,512]{2,0,1:T(8,128)(2,1)S(1)}, bf16[256,3,512]{2,0,1:T(8,128)(2,1)S(1)}, u32[]{:S(2)}, u32[]{:S(2)}) collective-permute-start(bf16[256,3,512]{2,0,1:T(8,128)(2,1)S(1)} %collective-permute-done.4), channel_id=1, source_target_pairs={{0,4},{4,8},{8,12},{12,16},{16,20},{20,24},{24,28},{28,0},{1,5},{5... | collective-permute-start | bytes 2359304 | tf_op jit(solution)/shard_map/ppermute | solution.py:24
  141.1 21.9 %copy-start.40 = (f32[3,512]{1,0:T(4,128)S(1)}, f32[3,512]{1,0:T(4,128)}, u32[]{:S(2)}) copy-start(f32[3,512]{1,0:T(4,128)} %param.17) | copy-start | bytes 18436
  213.2 188.0 %copy-start.41 = (f32[2048]{0:T(1024)S(1)}, f32[2048]{0:T(1024)}, u32[]{:S(2)}) copy-start(f32[2048]{0:T(1024)} %param.21) | copy-start | bytes 24580
  213.2 304.9 %reduce-scatter.15.cloned.1.call-start = ((), (), s32[]{:S(2)}) async-start(), calls=%async_computation.16 | async-start | bytes 2621440 | tf_op jit(solution)/shard_map/reduce_scatter | solution.py:244
  420.6 106.9 %reduce-scatter.9.cloned.1.call-start = ((), (), s32[]{:S(2)}) async-start(), calls=%async_computation.10 | async-start | bytes 5242880 | tf_op jit(solution)/shard_map/reduce_scatter | solution.py:171
  430.2 131.4 %reduce-scatter.11.cloned.1.call-start = ((), (), s32[]{:S(2)}) async-start(), calls=%async_computation.13 | async-start | bytes 2621440 | tf_op jit(solution)/shard_map/reduce_scatter | solution.py:173
  441.4 213.7 %reduce-scatter.19.cloned.1.call-start = ((), (), s32[]{:S(2)}) async-start(), calls=%async_computation.18 | async-start | bytes 4718592 | tf_op jit(solution)/shard_map/reduce_scatter | solution.py:183
  446.4 420.7 %reduce-scatter.17.cloned.1.call-start = ((), (), s32[]{:S(2)}) async-start(), calls=%async_computation.17 | async-start | bytes 14155776 | tf_op jit(solution)/shard_map/reduce_scatter | solution.py:264
  454.9 698.9 %reduce-scatter.23.cloned.1.call-start = ((), (), s32[]{:S(2)}) async-start(), calls=%async_computation.20 | async-start | bytes 18874368 | tf_op jit(solution)/shard_map/reduce_scatter | solution.py:184
  469.8 969.9 %reduce-scatter.21.cloned.1.call-start = ((), (), s32[]{:S(2)}) async-start(), calls=%async_computation.19 | async-start | bytes 18874368 | tf_op jit(solution)/shard_map/reduce_scatter | solution.py:265
  482.4 35.7 %copy-start.1 = (bf16[128,2048]{1,0:T(8,128)(2,1)S(1)}, bf16[128,2048]{1,0:T(8,128)(2,1)}, u32[]{:S(2)}) copy-start(bf16[128,2048]{1,0:T(8,128)(2,1)} %param.13) | copy-start | bytes 1572868
  482.4 35.7 %copy-start.24 = (f32[2048]{0:T(1024)S(1)}, f32[2048]{0:T(1024)}, u32[]{:S(2)}) copy-start(f32[2048]{0:T(1024)} %param.14) | copy-start | bytes 24580
  482.4 35.7 %copy-start.30 = (f32[128]{0:T(128)S(1)}, f32[128]{0:T(128)}, u32[]{:S(2)}) copy-start(f32[128]{0:T(128)} %copy-done.29) | copy-start | bytes 1540
  482.4 35.7 %copy-start.36 = (f32[128]{0:T(128)S(1)}, f32[128]{0:T(128)}, u32[]{:S(2)}) copy-start(f32[128]{0:T(128)} %copy-done.35) | copy-start | bytes 1540
  482.4 37.6 %copy-start.38 = (f32[128]{0:T(128)S(1)}, f32[128]{0:T(128)}, u32[]{:S(2)}) copy-start(f32[128]{0:T(128)} %copy-done.37) | copy-start | bytes 1540
  482.4 79.2 %copy-start.31 = (f32[2048]{0:T(1024)S(1)}, f32[2048]{0:T(1024)}, u32[]{:S(2)}) copy-start(f32[2048]{0:T(1024)} %param.23) | copy-start | bytes 24580
  482.4 79.2 %copy-start.32 = (f32[2048]{0:T(1024)S(1)}, f32[2048]{0:T(1024)}, u32[]{:S(2)}) copy-start(f32[2048]{0:T(1024)} %param.19) | copy-start | bytes 24580
  482.5 82.4 %copy-start.7 = (bf16[128,2048]{1,0:T(8,128)(2,1)S(1)}, bf16[128,2048]{1,0:T(8,128)(2,1)}, u32[]{:S(2)}) copy-start(bf16[128,2048]{1,0:T(8,128)(2,1)} %param.25) | copy-start | bytes 1572868
  607.9 832.4 %copy-start.34 = (f32[2048]{0:T(1024)}, f32[2048]{0:T(1024)S(1)}, u32[]{:S(2)}) copy-start(f32[2048]{0:T(1024)S(1)} %get-tuple-element.129) | copy-start | bytes 24580
  (31 other events, 117.1 us)
Sparse Core Ops, SparseCore 0:
  12.8 25.2 all-gather.5
  39.7 22.5 all-gather.13
  64.3 77.0 all-gather.7
  143.4 132.2 all-gather.9
  277.6 123.5 all-gather.11
  403.6 42.6 reduce-scatter.12
  449.0 31.4 reduce-scatter.14
  483.0 44.4 reduce-scatter.8
  530.2 31.4 reduce-scatter.10
  565.7 89.3 reduce-scatter.18
  659.7 207.4 reduce-scatter.16
  871.9 281.7 reduce-scatter.22
  1158.1 281.6 reduce-scatter.20
